TPU v7x, 256 devices: a whole 4x4x8 slice. The times are simulated.
256 devices in a mesh: tm: 8 (over y_hi, x), lat: 32 (over y_lo, z, core).
Axes of the slice: x: 4, y: 4 (y_hi: 2, y_lo: 2; y = y_hi * 2 + y_lo), z: 8, core: 2. Of those that a mesh axis runs over, the one named last changes fastest.
Arguments:
- frames: bfloat16 [128, 2048, 4096], P('tm', 'lat'), may hold values from -6 to 6
- owner_map: int32 [512], replicated, may hold values from 0 to 511, as said below
Outputs:
- spectrum: float32 [2, 512, 8, 1024], P(None, 'lat', None, 'tm')
Inputs may be any that keep to these rules, and one draw needn't show every extreme that they name: owner_map is a permutation of 0 to 511; entries 2 i and 2 i + 1 hold an order m and the order 512 - 1 - m.
All inputs are finite; a program needn't handle non-finite values.
Results may differ from a plain program's by a relative error of at most 0.0064.
Values may be sent and summed in bfloat16 or wider, within the bound.
A program may use at most 64 MiB of HBM per device.

v0:
```python
from functools import partial
import math

import jax
import jax.numpy as jnp
from jax import lax
from jax.experimental import pallas as pl
from jax.experimental.pallas import tpu as pltpu
from jax.sharding import PartitionSpec as P
import ml_dtypes
import numpy as np

L = 1024
F = 8
BF16 = jnp.bfloat16
F32 = jnp.float32


def longitude_tables(nlon, orders):
    half = nlon // 2
    points = np.arange(half, dtype=np.int64)[:, None]
    factor = math.sqrt(2.0 / nlon)
    tables = []
    for parity in range(2):
        order = np.arange(parity, orders, 2, dtype=np.int64)[None, :]
        angles = (points * order % nlon) * (2.0 * math.pi / nlon)
        tables.append(np.concatenate([np.cos(angles) * factor, -np.sin(angles) * factor], axis=1))
    return np.stack(tables).astype(np.float32).astype(ml_dtypes.bfloat16)


def time_tables(parts, frames, rows):
    total = parts * frames
    times = np.arange(total, dtype=np.int64)[None, :]
    frequency = (total // 8 + np.arange(F, dtype=np.int64))[:, None]
    angles = (frequency * times % total) * (2.0 * math.pi / total)
    cos_part = np.cos(angles) / math.sqrt(total)
    sin_part = np.sin(angles) / math.sqrt(total)
    real = np.concatenate([cos_part, -sin_part], axis=0)
    imag = np.concatenate([sin_part, cos_part], axis=0)
    table = np.stack([real, imag]).reshape(2, 2 * F, parts, frames).transpose(2, 0, 1, 3)
    wide = table[:, :, :, None, :, None] * np.eye(rows)[None, None, None, :, None, :]
    wide = wide.reshape(parts, 2, 2 * F * rows, frames * rows)
    return wide.astype(np.float32).astype(ml_dtypes.bfloat16)


def band_kernel(part_ref, frames_ref, tab_ref, wk_ref, own_ref, out_ref, bc_ref, ot_ref, oh_ref):
    step = pl.program_id(0)
    frame_count, rows, nlon = frames_ref.shape
    half = nlon // 2
    orders = own_ref.shape[1]
    pairs = orders // 2
    image = frames_ref[...].reshape(frame_count * rows, nlon)
    first, second = image[:, :half], image[:, half:]
    for parity in range(2):
        folded = first + second if parity == 0 else first - second
        coef = jnp.dot(folded, tab_ref[parity], preferred_element_type=F32).astype(BF16)
        part = jnp.dot(wk_ref[0, 0], coef[:, :pairs], preferred_element_type=F32)
        part = part + jnp.dot(wk_ref[0, 1], coef[:, pairs:], preferred_element_type=F32)
        row = pl.multiple_of(step * rows, rows)
        bc_ref[:, pl.ds(row, rows), parity * pairs : (parity + 1) * pairs] = part.astype(
            BF16
        ).reshape(2 * F, rows, pairs)

    @pl.when(step == 0)
    def _():
        wide = jnp.broadcast_to(own_ref[...].astype(F32), (128, orders))
        for block in range(orders // 128):
            ot_ref[block * 128 : (block + 1) * 128, :] = wide[:, block * 128 : (block + 1) * 128].T
        lane = lax.broadcasted_iota(jnp.int32, (32, orders), 1)
        order = jnp.where(lane < pairs, 2 * lane, 2 * (lane - pairs) + 1).astype(F32)
        for slot in range(2):
            for peer in range(8):
                held = ot_ref[pl.ds(2 * peer + slot, 32, stride=16), :]
                held = jnp.concatenate([held] * (orders // 128), axis=1)
                at = (slot * 8 + peer) * 32
                oh_ref[at : at + 32, :] = jnp.where(held == order, 1.0, 0.0).astype(BF16)

    @pl.when(step == pl.num_programs(0) - 1)
    def _():
        lat_rows = bc_ref.shape[1]
        flat = bc_ref[...].reshape(2 * F * lat_rows, orders)
        moved = [
            lax.dot_general(
                oh_ref[slot * pairs : (slot + 1) * pairs, :],
                flat,
                (((1,), (1,)), ((), ())),
                preferred_element_type=F32,
            ).astype(BF16)
            for slot in range(2)
        ]
        for ef in range(2 * F):
            at = slice(ef * lat_rows, (ef + 1) * lat_rows)
            out_ref[:, ef * 128 : (ef + 1) * 128] = jnp.concatenate(
                [moved[0][:, at], moved[1][:, at]], axis=1
            )


def partial_band(frames, owner_map, parts):
    frame_count, lat_rows, nlon = frames.shape
    orders = owner_map.shape[0]
    rows = 16
    tab = jnp.asarray(longitude_tables(nlon, orders))
    wk = jnp.asarray(time_tables(parts, frame_count, rows))
    size = frame_count * rows
    part = lax.axis_index("tm").astype(jnp.int32).reshape(1)
    return pl.pallas_call(
        band_kernel,
        out_shape=jax.ShapeDtypeStruct((orders // 2, 2 * F * 128), BF16),
        grid_spec=pltpu.PrefetchScalarGridSpec(
            num_scalar_prefetch=1,
            grid=(lat_rows // rows,),
            in_specs=[
                pl.BlockSpec((frame_count, rows, nlon), lambda i, part: (0, i, 0)),
                pl.BlockSpec((2, nlon // 2, orders), lambda i, part: (0, 0, 0), pipeline_mode=pl.Buffered(1)),
                pl.BlockSpec((1, 2, size, size), lambda i, part: (part[0], 0, 0, 0), pipeline_mode=pl.Buffered(1)),
                pl.BlockSpec((1, orders), lambda i, part: (0, 0)),
            ],
            out_specs=pl.BlockSpec((orders // 2, 2 * F * 128), lambda i, part: (0, 0)),
            scratch_shapes=[
                pltpu.VMEM((2 * F, lat_rows, orders), BF16),
                pltpu.VMEM((orders, 128), F32),
                pltpu.VMEM((orders, orders), BF16),
            ],
        ),
        compiler_params=pltpu.CompilerParams(
            dimension_semantics=("arbitrary",), vmem_limit_bytes=48 << 20
        ),
        name="partial_band",
    )(part, frames, tab, wk, owner_map.reshape(1, orders))


def latitude_constants(nlat, lat_rows):
    colatitude = (np.arange(nlat) + 0.5) * (math.pi / nlat)
    sine = np.sin(colatitude)
    weight = sine * (math.pi / nlat) * math.sqrt(nlat)

    def lay(values):
        values = values.reshape(nlat // lat_rows, lat_rows)
        return np.concatenate([values, values], axis=1)

    steps = np.log1p(0.5 / np.arange(1, 1025)).reshape(8, 128)
    grids = np.stack([lay(np.cos(colatitude)), lay(np.log(sine)), lay(weight)])
    return grids.astype(np.float32), steps.astype(np.float32)


def degree_factors(order, rise_ref, fall_ref):
    block = 64

    def body(i, carry):
        at = pl.multiple_of(i * block, block)
        level = (at + lax.broadcasted_iota(jnp.int32, (block, 128), 0)).astype(F32)
        level_sq = level * level
        order_sq = order * order
        lower = level - 1.0
        rising = jnp.sqrt(
            jnp.maximum(4.0 * level_sq - 1.0, 0.0) / jnp.maximum(level_sq - order_sq, 1.0)
        )
        falling = jnp.sqrt(
            jnp.maximum(lower * lower - order_sq, 0.0)
            / jnp.maximum(4.0 * lower * lower - 1.0, 1.0)
        )
        rise_ref[pl.ds(at, block), :] = rising
        fall_ref[pl.ds(at, block), :] = rising * falling
        return carry

    lax.fori_loop(0, L // block, body, 0)


def diagonal(order, grids_ref, steps_ref, held):
    step = (
        128 * lax.broadcasted_iota(jnp.int32, (8, 128), 0)
        + lax.broadcasted_iota(jnp.int32, (8, 128), 1)
        + 1
    )
    sums = [
        jnp.sum(jnp.where(step <= m, steps_ref[...], 0.0), axis=(0, 1), keepdims=True) for m in held
    ]
    lane = lax.broadcasted_iota(jnp.int32, (1, 128), 1)
    growth = jnp.where(lane < 64, sums[0], sums[1])
    lognorm = 0.5 * math.log(0.5) + 0.5 * growth + order * grids_ref[1]
    start = jnp.where(lognorm >= -60.0, jnp.exp(jnp.maximum(lognorm, -60.0)), 0.0)
    return start * grids_ref[2]


def fill_table(order, start, cosine, rise_ref, fall_ref, stage_ref, table_ref, lo, hi, state):
    groups = start.shape[0] // 8
    span = 16

    def body(i, carry):
        base = pl.multiple_of(i * span, span)
        newer, older = list(carry[0]), list(carry[1])
        for k in range(span):
            rise = jnp.broadcast_to(rise_ref[pl.ds(base + k, 1), :], (8, 128))
            fall = jnp.broadcast_to(fall_ref[pl.ds(base + k, 1), :], (8, 128))
            first = jnp.broadcast_to(order, (8, 128)) == (base + k).astype(F32)
            for g in range(groups):
                at = slice(8 * g, 8 * g + 8)
                now = (rise * cosine[at]) * newer[g] - fall * older[g]
                now = jnp.where(first, start[at], now)
                newer[g], older[g] = now, newer[g]
                stage_ref[(g * span + k) * 8 : (g * span + k) * 8 + 8, :] = now
        for g in range(groups):
            for j in range(8):
                rows = stage_ref[pl.ds(g * span * 8 + j, span, stride=8), :]
                table_ref[pl.ds(base, span), (8 * g + j) * 128 : (8 * g + j + 1) * 128] = (
                    rows.astype(BF16)
                )
        return tuple(newer), tuple(older)

    return lax.fori_loop(lo // span, hi // span, body, state)


def spectrum_kernel(first_ref, own_ref, band_ref, grids_ref, steps_ref, out_ref, rise_ref, fall_ref, stage_ref, table_ref, both_ref):
    m0 = own_ref[first_ref[0]]
    m1 = own_ref[first_ref[0] + 1]
    lane = lax.broadcasted_iota(jnp.int32, (1, 128), 1)
    order = jnp.where(lane < 64, m0, m1).astype(F32)
    degree_factors(order, rise_ref, fall_ref)
    start = diagonal(order, grids_ref, steps_ref, (m0, m1))
    cosine = grids_ref[0]
    count = start.shape[0]
    zeros = tuple(jnp.zeros((8, 128), F32) for _ in range(count // 8))
    fill_table(order, start, cosine, rise_ref, fall_ref, stage_ref, table_ref, 0, L, (zeros, zeros))
    lanes = lax.broadcasted_iota(jnp.int32, (16, 128), 1)
    for j in range(count):
        tile = band_ref[j]
        zero = jnp.zeros_like(tile)
        both_ref[0:16, j * 128 : (j + 1) * 128] = jnp.where(lanes < 64, tile, zero)
        both_ref[16:32, j * 128 : (j + 1) * 128] = jnp.where(lanes < 64, zero, tile)
    for q in range(L // 128):
        out_ref[q] = lax.dot_general(
            both_ref[...],
            table_ref[q * 128 : (q + 1) * 128, :],
            (((1,), (1,)), ((), ())),
            preferred_element_type=F32,
        )


def spectrum(band, owner_map, first_slot, nlat):
    groups = band.shape[0]
    grids, steps = latitude_constants(nlat, nlat // groups)
    vmem = pl.BlockSpec(memory_space=pltpu.VMEM)
    smem = pl.BlockSpec(memory_space=pltpu.SMEM)
    return pl.pallas_call(
        spectrum_kernel,
        out_shape=jax.ShapeDtypeStruct((L // 128, 4 * F, 128), F32),
        in_specs=[smem, smem, vmem, vmem, vmem],
        out_specs=vmem,
        scratch_shapes=[
            pltpu.VMEM((L, 128), F32),
            pltpu.VMEM((L, 128), F32),
            pltpu.VMEM((groups * 16, 128), F32),
            pltpu.VMEM((L, groups * 128), BF16),
            pltpu.VMEM((4 * F, groups * 128), BF16),
        ],
        compiler_params=pltpu.CompilerParams(vmem_limit_bytes=48 << 20),
        name="spectrum",
    )(first_slot.reshape(1), owner_map, band, jnp.asarray(grids), jnp.asarray(steps))


def shards(frames, owner_map):
    lat_count = lax.axis_size("lat")
    time_count = lax.axis_size("tm")
    orders = owner_map.shape[0]
    sent = partial_band(frames, owner_map, time_count)
    sent = sent.reshape(time_count, lat_count, 2 * F * 128)
    parts = lax.all_to_all(sent, "tm", split_axis=0, concat_axis=0, tiled=True)
    total = jnp.sum(parts.astype(F32), axis=0).astype(BF16).reshape(lat_count, 2 * F, 128)
    band = lax.all_to_all(total, "lat", split_axis=0, concat_axis=0, tiled=True)
    first_slot = lax.axis_index("lat") * (orders // lat_count) + lax.axis_index("tm") * 2
    pieces = spectrum(band, owner_map, first_slot.astype(jnp.int32), lat_count * frames.shape[1])
    pieces = lax.all_to_all(pieces, "tm", split_axis=0, concat_axis=0, tiled=True)
    pieces = pieces.reshape(time_count, 2, 2, F, 128).transpose(2, 0, 1, 3, 4)
    return pieces.reshape(2, 2 * time_count, F, 128)


def solution(mesh):
    return jax.shard_map(
        shards,
        mesh=mesh,
        in_specs=(P("tm", "lat", None), P()),
        out_specs=P(None, "lat", None, "tm"),
        check_vma=False,
    )
```

profile of v0, /device:TPU:1, one launch (start us, length us, event | category | flops | bytes accessed | tf_op | source)
XLA Modules:
  0.0 78.3 jit_solution(7996356460152189790)
XLA Ops:
  0.0 0.0 copy-start
  0.0 1.6 %copy-done = bf16[8,2,256,256]{3,2,1,0:T(8,128)(2,1)S(1)} copy-done((bf16[8,2,256,256]{3,2,1,0:T(8,128)(2,1)S(1)}, bf16[8,2,256,256]{3,2,1,0:T(8,128)(2,1)}, u32[]{:S(2)}) %copy-start) | copy-done | bytes 2097176
  1.6 0.0 copy-start.2
  1.6 0.7 copy-done.2
  2.3 0.0 copy-start.1
  2.3 0.0 copy-start.3
  2.3 0.0 copy-start.4
  2.3 11.0 %partial_band.1 = bf16[256,2048]{1,0:T(8,128)(2,1)S(1)} custom-call(s32[1]{0:T(128)} %bitcast.1.part_ref, bf16[16,64,4096]{2,1,0:T(8,128)(2,1)} %frames_ref.1, bf16[2,2048,512]{2,1,0:T(8,128)(2,1)} %constant.24.clone.tab_ref, bf16[8,2,256,256]{3,2,1,0:T(8,128)(2,1)S(1)} %copy-done, s32[1,512]{1,0:T(1,128)S(1)} %bitcast.11), custom_call_target="tpu_custom_call" | custom-call | tf_op jit(solution)/shard_map/partial_band/pallas_call | solution.py:106
  13.3 23.6 %all_to_all.15 = bf16[8,32,2048]{2,1,0:T(8,128)(2,1)S(1)} all-to-all(bf16[8,32,2048]{2,1,0:T(8,128)(2,1)S(1)} %bitcast.10), channel_id=1, replica_groups=mesh['tm'=8,'lat'=32] {'tm'}, dimensions={0} | all-to-all | bytes 2097152 | tf_op jit(solution)/shard_map/all_to_all | solution.py:267
  36.9 0.1 reduce_sum.12
  37.1 0.7 copy.8
  37.7 10.6 %all-to-all-start.1 = ((bf16[32,16,128]{2,1,0:T(8,128)(2,1)}), bf16[32,16,128]{2,1,0:T(8,128)(2,1)S(1)}, u32[]{:S(2)}, u32[]{:S(2)}) async-start(bf16[32,16,128]{2,1,0:T(8,128)(2,1)} %bitcast.9), calls=%async_computation.1 | async-start | bytes 262144 | tf_op jit(solution)/shard_map/all_to_all | solution.py:269
  48.3 9.1 %all-to-all-done.1.band_ref = bf16[32,16,128]{2,1,0:T(8,128)(2,1)S(1)} async-done(((bf16[32,16,128]{2,1,0:T(8,128)(2,1)}), bf16[32,16,128]{2,1,0:T(8,128)(2,1)S(1)}, u32[]{:S(2)}, u32[]{:S(2)}) %all-to-all-start.1) | async-done | bytes 131104 | tf_op jit(solution)/shard_map/all_to_all | solution.py:269
  57.4 0.0 copy-done.1
  57.4 0.0 copy-done.3
  57.4 0.0 copy-done.4
  57.4 10.3 %spectrum.1 = f32[8,32,128]{2,1,0:T(8,128)S(1)} custom-call(s32[1]{0:T(128)} %bitcast.first_ref, s32[512]{0:T(512)S(1)} %copy-done.3, bf16[32,16,128]{2,1,0:T(8,128)(2,1)S(1)} %all-to-all-done.1.band_ref, f32[3,32,128]{2,1,0:T(8,128)S(1)} %copy-done.1, f32[8,128]{1,0:T(8,128)S(1)} %copy-done.4), custom_call_target="tpu_custom_call" | custom-call | tf_op jit(solution)/shard_map/spectrum/pallas_call | solution.py:244
  67.7 9.9 %all_to_all.16 = f32[8,32,128]{2,1,0:T(8,128)S(1)} all-to-all(f32[8,32,128]{2,1,0:T(8,128)S(1)} %spectrum.1), channel_id=1, replica_groups=mesh['tm'=8,'lat'=32] {'tm'}, dimensions={0} | all-to-all | bytes 262144 | tf_op jit(solution)/shard_map/all_to_all | solution.py:272
  77.6 0.7 copy.7
Async XLA Ops:
  0.0 1.6 %copy-start = (bf16[8,2,256,256]{3,2,1,0:T(8,128)(2,1)S(1)}, bf16[8,2,256,256]{3,2,1,0:T(8,128)(2,1)}, u32[]{:S(2)}) copy-start(bf16[8,2,256,256]{3,2,1,0:T(8,128)(2,1)} %constant.25.clone.wk_ref) | copy-start | bytes 6291460
  1.6 0.7 copy-start.2
  2.3 55.1 %copy-start.1 = (f32[3,32,128]{2,1,0:T(8,128)S(1)}, f32[3,32,128]{2,1,0:T(8,128)}, u32[]{:S(2)}) copy-start(f32[3,32,128]{2,1,0:T(8,128)} %constant.26.clone.grids_ref) | copy-start | bytes 147460
  2.3 55.1 %copy-start.3 = (s32[512]{0:T(512)S(1)}, s32[512]{0:T(512)}, u32[]{:S(2)}) copy-start(s32[512]{0:T(512)} %own_ref.1) | copy-start | bytes 6148
  2.3 55.1 %copy-start.4 = (f32[8,128]{1,0:T(8,128)S(1)}, f32[8,128]{1,0:T(8,128)}, u32[]{:S(2)}) copy-start(f32[8,128]{1,0:T(8,128)} %constant.27.clone.steps_ref) | copy-start | bytes 12292
  37.7 19.7 %all-to-all-start.1 = ((bf16[32,16,128]{2,1,0:T(8,128)(2,1)}), bf16[32,16,128]{2,1,0:T(8,128)(2,1)S(1)}, u32[]{:S(2)}, u32[]{:S(2)}) async-start(bf16[32,16,128]{2,1,0:T(8,128)(2,1)} %bitcast.9), calls=%async_computation.1 | async-start | bytes 262144 | tf_op jit(solution)/shard_map/all_to_all | solution.py:269
where the time goes:
time: 79.5 us; the launch traced here: 78.3 us
  blocking collectives  33.5 us (42%)
  Pallas kernels  21.4 us (27%)
  starting transfers between devices  10.6 us (13%)
  waiting for transfers between devices  9.06 us (11%)
  local copies, waits for them, and re-layouts  3.62 us (5%)
    all_to_all x1, blocking collectives, shards(): parts = lax.all_to_all(sent, 'tm', split_axis=0, concat_axis=0, tiled=True)  23.6 us
    pallas_call x1, Pallas kernels, partial_band(): pl.pallas_call(band_kernel, out_shape=jax.ShapeDtypeStruct((orders // 2,...  11 us
    all_to_all x1, starting transfers between devices, shards(): band = lax.all_to_all(total, 'lat', split_axis=0, concat_axis=0, tiled=True)  10.6 us
    pallas_call x1, Pallas kernels, spectrum(): pl.pallas_call(spectrum_kernel, out_shape=jax.ShapeDtypeStruct((L // 128,...  10.3 us
    all_to_all x1, blocking collectives, shards(): lax.all_to_all(pieces, 'tm', split_axis=0, concat_axis=0, tiled=True)  9.89 us
    all_to_all x1, waiting for transfers between devices, shards(): band = lax.all_to_all(total, 'lat', split_axis=0, concat_axis=0, tiled=True)  9.06 us
    unnamed x11, local copies, waits for them, and re-layouts  2.96 us
  transfers between devices with their start and end apart: 1, of which 1 were waited for; matrix products, arithmetic and copies ran while one was open for 0% of the time, Pallas kernels for 0%

commit v1 on v0

--- a/solution.py
+++ b/solution.py
@@ -7,25 +7,27 @@
 from jax.experimental import pallas as pl
 from jax.experimental.pallas import tpu as pltpu
 from jax.sharding import PartitionSpec as P
-import ml_dtypes
 import numpy as np
 
 L = 1024
 F = 8
 BF16 = jnp.bfloat16
+MESH = pl.DeviceIdType.MESH
 F32 = jnp.float32
 
 
-def longitude_tables(nlon, orders):
-    half = nlon // 2
-    points = np.arange(half, dtype=np.int64)[:, None]
-    factor = math.sqrt(2.0 / nlon)
-    tables = []
+def longitude_seeds(nlon, orders, fine):
+    count = nlon // 2 // fine
+    coarse, near = [], []
     for parity in range(2):
         order = np.arange(parity, orders, 2, dtype=np.int64)[None, :]
-        angles = (points * order % nlon) * (2.0 * math.pi / nlon)
-        tables.append(np.concatenate([np.cos(angles) * factor, -np.sin(angles) * factor], axis=1))
-    return np.stack(tables).astype(np.float32).astype(ml_dtypes.bfloat16)
+        for points, scale, out in (
+            (np.arange(count, dtype=np.int64)[:, None] * fine, math.sqrt(2.0 / nlon), coarse),
+            (np.arange(fine, dtype=np.int64)[:, None], 1.0, near),
+        ):
+            angles = (points * order % nlon) * (2.0 * math.pi / nlon)
+            out.append(np.stack([np.cos(angles) * scale, np.sin(angles) * scale]))
+    return np.stack(coarse).astype(np.float32), np.stack(near).astype(np.float32)
 
 
 def time_tables(parts, frames, rows):
@@ -38,31 +40,42 @@
     real = np.concatenate([cos_part, -sin_part], axis=0)
     imag = np.concatenate([sin_part, cos_part], axis=0)
     table = np.stack([real, imag]).reshape(2, 2 * F, parts, frames).transpose(2, 0, 1, 3)
-    wide = table[:, :, :, None, :, None] * np.eye(rows)[None, None, None, :, None, :]
-    wide = wide.reshape(parts, 2, 2 * F * rows, frames * rows)
-    return wide.astype(np.float32).astype(ml_dtypes.bfloat16)
-
-
-def band_kernel(part_ref, frames_ref, tab_ref, wk_ref, own_ref, out_ref, bc_ref, ot_ref, oh_ref):
+    return np.repeat(table, rows, axis=3).astype(np.float32)
+
+
+def band_kernel(
+    part_ref, frames_ref, coarse_ref, near_ref, time_ref, own_ref, out_ref,
+    tab_ref, wk_ref, bc_ref, ot_ref, oh_ref,
+):
     step = pl.program_id(0)
     frame_count, rows, nlon = frames_ref.shape
     half = nlon // 2
     orders = own_ref.shape[1]
     pairs = orders // 2
-    image = frames_ref[...].reshape(frame_count * rows, nlon)
-    first, second = image[:, :half], image[:, half:]
-    for parity in range(2):
-        folded = first + second if parity == 0 else first - second
-        coef = jnp.dot(folded, tab_ref[parity], preferred_element_type=F32).astype(BF16)
-        part = jnp.dot(wk_ref[0, 0], coef[:, :pairs], preferred_element_type=F32)
-        part = part + jnp.dot(wk_ref[0, 1], coef[:, pairs:], preferred_element_type=F32)
-        row = pl.multiple_of(step * rows, rows)
-        bc_ref[:, pl.ds(row, rows), parity * pairs : (parity + 1) * pairs] = part.astype(
-            BF16
-        ).reshape(2 * F, rows, pairs)
 
     @pl.when(step == 0)
     def _():
+        fine = near_ref.shape[2]
+        for parity in range(2):
+
+            def body(i, carry):
+                cos_row = coarse_ref[parity, 0, pl.ds(i, 1), :]
+                sin_row = coarse_ref[parity, 1, pl.ds(i, 1), :]
+                near_cos, near_sin = near_ref[parity, 0], near_ref[parity, 1]
+                at = pl.ds(pl.multiple_of(i * fine, fine), fine)
+                tab_ref[parity, at, :pairs] = (cos_row * near_cos - sin_row * near_sin).astype(BF16)
+                tab_ref[parity, at, pairs:] = (-sin_row * near_cos - cos_row * near_sin).astype(BF16)
+                return carry
+
+            lax.fori_loop(0, half // fine, body, 0)
+        size = frame_count * rows
+        same = lax.broadcasted_iota(jnp.int32, (rows, size), 0) == lax.rem(
+            lax.broadcasted_iota(jnp.int32, (rows, size), 1), rows
+        )
+        for c in range(2):
+            for ef in range(2 * F):
+                line = jnp.broadcast_to(time_ref[0, c, ef : ef + 1, :], (rows, size))
+                wk_ref[c, ef * rows : (ef + 1) * rows, :] = jnp.where(same, line, 0.0).astype(BF16)
         wide = jnp.broadcast_to(own_ref[...].astype(F32), (128, orders))
         for block in range(orders // 128):
             ot_ref[block * 128 : (block + 1) * 128, :] = wide[:, block * 128 : (block + 1) * 128].T
@@ -74,6 +87,18 @@
                 held = jnp.concatenate([held] * (orders // 128), axis=1)
                 at = (slot * 8 + peer) * 32
                 oh_ref[at : at + 32, :] = jnp.where(held == order, 1.0, 0.0).astype(BF16)
+
+    image = frames_ref[...].reshape(frame_count * rows, nlon)
+    first, second = image[:, :half], image[:, half:]
+    for parity in range(2):
+        folded = first + second if parity == 0 else first - second
+        coef = jnp.dot(folded, tab_ref[parity], preferred_element_type=F32).astype(BF16)
+        part = jnp.dot(wk_ref[0], coef[:, :pairs], preferred_element_type=F32)
+        part = part + jnp.dot(wk_ref[1], coef[:, pairs:], preferred_element_type=F32)
+        row = pl.multiple_of(step * rows, rows)
+        bc_ref[:, pl.ds(row, rows), parity * pairs : (parity + 1) * pairs] = part.astype(
+            BF16
+        ).reshape(2 * F, rows, pairs)
 
     @pl.when(step == pl.num_programs(0) - 1)
     def _():
@@ -98,11 +123,12 @@
 def partial_band(frames, owner_map, parts):
     frame_count, lat_rows, nlon = frames.shape
     orders = owner_map.shape[0]
-    rows = 16
-    tab = jnp.asarray(longitude_tables(nlon, orders))
-    wk = jnp.asarray(time_tables(parts, frame_count, rows))
+    rows, fine = 16, 64
+    coarse, near = longitude_seeds(nlon, orders, fine)
+    table = time_tables(parts, frame_count, rows)
     size = frame_count * rows
     part = lax.axis_index("tm").astype(jnp.int32).reshape(1)
+    once = pl.Buffered(1)
     return pl.pallas_call(
         band_kernel,
         out_shape=jax.ShapeDtypeStruct((orders // 2, 2 * F * 128), BF16),
@@ -111,12 +137,15 @@
             grid=(lat_rows // rows,),
             in_specs=[
                 pl.BlockSpec((frame_count, rows, nlon), lambda i, part: (0, i, 0)),
-                pl.BlockSpec((2, nlon // 2, orders), lambda i, part: (0, 0, 0), pipeline_mode=pl.Buffered(1)),
-                pl.BlockSpec((1, 2, size, size), lambda i, part: (part[0], 0, 0, 0), pipeline_mode=pl.Buffered(1)),
+                pl.BlockSpec(coarse.shape, lambda i, part: (0, 0, 0, 0), pipeline_mode=once),
+                pl.BlockSpec(near.shape, lambda i, part: (0, 0, 0, 0), pipeline_mode=once),
+                pl.BlockSpec((1,) + table.shape[1:], lambda i, part: (part[0], 0, 0, 0), pipeline_mode=once),
                 pl.BlockSpec((1, orders), lambda i, part: (0, 0)),
             ],
             out_specs=pl.BlockSpec((orders // 2, 2 * F * 128), lambda i, part: (0, 0)),
             scratch_shapes=[
+                pltpu.VMEM((2, nlon // 2, orders), BF16),
+                pltpu.VMEM((2, size, size), BF16),
                 pltpu.VMEM((2 * F, lat_rows, orders), BF16),
                 pltpu.VMEM((orders, 128), F32),
                 pltpu.VMEM((orders, orders), BF16),
@@ -126,7 +155,7 @@
             dimension_semantics=("arbitrary",), vmem_limit_bytes=48 << 20
         ),
         name="partial_band",
-    )(part, frames, tab, wk, owner_map.reshape(1, orders))
+    )(part, frames, jnp.asarray(coarse), jnp.asarray(near), jnp.asarray(table), owner_map.reshape(1, orders))
 
 
 def latitude_constants(nlat, lat_rows):
@@ -210,68 +239,184 @@
     return lax.fori_loop(lo // span, hi // span, body, state)
 
 
-def spectrum_kernel(first_ref, own_ref, band_ref, grids_ref, steps_ref, out_ref, rise_ref, fall_ref, stage_ref, table_ref, both_ref):
-    m0 = own_ref[first_ref[0]]
-    m1 = own_ref[first_ref[0] + 1]
+def exchange_kernel(
+    own_ref, sent_ref, grids_ref, steps_ref, out_ref,
+    rise_ref, fall_ref, stage_ref, table_ref, both_ref,
+    parts_ref, sum_ref, away_ref, band_ref, gone_ref, degrees_ref,
+    part_send, part_recv, lat_send, lat_recv, deg_send, deg_recv,
+):
+    tm, lat = lax.axis_index("tm"), lax.axis_index("lat")
+    time_count, lat_count = parts_ref.shape[0], band_ref.shape[0]
+
+    def time_peer(d):
+        return lax.rem(tm + d, time_count)
+
+    def lat_peer(d):
+        return lax.rem(lat + d, lat_count)
+
+    barrier = pltpu.get_barrier_semaphore()
+
+    def greet_time(d, carry):
+        pl.semaphore_signal(barrier, inc=1, device_id={"tm": time_peer(d)}, device_id_type=MESH)
+        return carry
+
+    def greet_lat(d, carry):
+        pl.semaphore_signal(barrier, inc=1, device_id={"lat": lat_peer(d)}, device_id_type=MESH)
+        return carry
+
+    lax.fori_loop(1, time_count, greet_time, 0)
+    lax.fori_loop(1, lat_count, greet_lat, 0)
+    pl.semaphore_wait(barrier, time_count + lat_count - 2)
+
+    def part_copy(d):
+        return pltpu.make_async_remote_copy(
+            src_ref=sent_ref.at[time_peer(d)], dst_ref=parts_ref.at[tm],
+            send_sem=part_send.at[d], recv_sem=part_recv.at[tm],
+            device_id={"tm": time_peer(d)}, device_id_type=MESH,
+        )
+
+    def part_arrival(d):
+        peer = time_peer(d)
+        return pltpu.make_async_remote_copy(
+            src_ref=sent_ref.at[peer], dst_ref=parts_ref.at[peer],
+            send_sem=part_send.at[d], recv_sem=part_recv.at[peer],
+            device_id={"tm": peer}, device_id_type=MESH,
+        )
+
+    def band_copy(d):
+        return pltpu.make_async_remote_copy(
+            src_ref=away_ref.at[lat_peer(d)], dst_ref=band_ref.at[lat],
+            send_sem=lat_send.at[d], recv_sem=lat_recv.at[lat],
+            device_id={"lat": lat_peer(d)}, device_id_type=MESH,
+        )
+
+    def band_arrival(d):
+        peer = lat_peer(d)
+        return pltpu.make_async_remote_copy(
+            src_ref=away_ref.at[peer], dst_ref=band_ref.at[peer],
+            send_sem=lat_send.at[d], recv_sem=lat_recv.at[peer],
+            device_id={"lat": peer}, device_id_type=MESH,
+        )
+
+    def degree_copy(d):
+        return pltpu.make_async_remote_copy(
+            src_ref=gone_ref.at[time_peer(d)], dst_ref=degrees_ref.at[tm],
+            send_sem=deg_send.at[d], recv_sem=deg_recv.at[tm],
+            device_id={"tm": time_peer(d)}, device_id_type=MESH,
+        )
+
+    def degree_arrival(d):
+        peer = time_peer(d)
+        return pltpu.make_async_remote_copy(
+            src_ref=gone_ref.at[peer], dst_ref=degrees_ref.at[peer],
+            send_sem=deg_send.at[d], recv_sem=deg_recv.at[peer],
+            device_id={"tm": peer}, device_id_type=MESH,
+        )
+
+    def run(first, last, action):
+        def body(d, carry):
+            action(d)
+            return carry
+
+        lax.fori_loop(first, last, body, 0)
+
+    run(1, time_count, lambda d: part_copy(d).start())
+
+    slot = lat * (2 * time_count) + tm * 2
+    m0, m1 = own_ref[slot], own_ref[slot + 1]
     lane = lax.broadcasted_iota(jnp.int32, (1, 128), 1)
     order = jnp.where(lane < 64, m0, m1).astype(F32)
     degree_factors(order, rise_ref, fall_ref)
     start = diagonal(order, grids_ref, steps_ref, (m0, m1))
-    cosine = grids_ref[0]
-    count = start.shape[0]
-    zeros = tuple(jnp.zeros((8, 128), F32) for _ in range(count // 8))
-    fill_table(order, start, cosine, rise_ref, fall_ref, stage_ref, table_ref, 0, L, (zeros, zeros))
-    lanes = lax.broadcasted_iota(jnp.int32, (16, 128), 1)
-    for j in range(count):
+    zeros = tuple(jnp.zeros((8, 128), F32) for _ in range(lat_count // 8))
+    fill_table(
+        order, start, grids_ref[0], rise_ref, fall_ref, stage_ref, table_ref, 0, L, (zeros, zeros)
+    )
+
+    run(1, time_count, lambda d: part_arrival(d).wait_recv())
+    for ef in range(2 * F):
+        at = slice(ef * 128, (ef + 1) * 128)
+        total = sent_ref[tm, :, at].astype(F32)
+        for d in range(1, time_count):
+            total = total + parts_ref[time_peer(d), :, at].astype(F32)
+        sum_ref[pl.ds(ef, lat_count, stride=2 * F), :] = total
+    away_ref[...] = sum_ref[...].astype(BF16).reshape(away_ref.shape)
+    run(1, lat_count, lambda d: band_copy(d).start())
+    band_ref[lat] = away_ref[lat]
+    run(1, lat_count, lambda d: band_arrival(d).wait_recv())
+
+    lanes = lax.broadcasted_iota(jnp.int32, (2 * F, 128), 1)
+    for j in range(lat_count):
         tile = band_ref[j]
         zero = jnp.zeros_like(tile)
-        both_ref[0:16, j * 128 : (j + 1) * 128] = jnp.where(lanes < 64, tile, zero)
-        both_ref[16:32, j * 128 : (j + 1) * 128] = jnp.where(lanes < 64, zero, tile)
-    for q in range(L // 128):
-        out_ref[q] = lax.dot_general(
+        at = slice(j * 128, (j + 1) * 128)
+        both_ref[0 : 2 * F, at] = jnp.where(lanes < 64, tile, zero)
+        both_ref[2 * F : 4 * F, at] = jnp.where(lanes < 64, zero, tile)
+
+    def piece(q):
+        return lax.dot_general(
             both_ref[...],
-            table_ref[q * 128 : (q + 1) * 128, :],
+            table_ref[pl.ds(pl.multiple_of(q * 128, 128), 128), :],
             (((1,), (1,)), ((), ())),
             preferred_element_type=F32,
         )
 
-
-def spectrum(band, owner_map, first_slot, nlat):
-    groups = band.shape[0]
-    grids, steps = latitude_constants(nlat, nlat // groups)
+    def send_piece(d):
+        gone_ref[time_peer(d)] = piece(time_peer(d))
+        degree_copy(d).start()
+
+    run(1, time_count, send_piece)
+    degrees_ref[tm] = piece(tm)
+    run(1, time_count, lambda d: degree_arrival(d).wait_recv())
+    for peer in range(time_count):
+        for slot in range(2):
+            for e in range(2):
+                out_ref[e, 2 * peer + slot] = degrees_ref[peer, (2 * slot + e) * F : (2 * slot + e + 1) * F, :]
+    run(1, time_count, lambda d: part_copy(d).wait_send())
+    run(1, lat_count, lambda d: band_copy(d).wait_send())
+    run(1, time_count, lambda d: degree_copy(d).wait_send())
+
+
+def exchange(sent, owner_map, nlat):
+    time_count, lat_count, width = sent.shape
+    grids, steps = latitude_constants(nlat, nlat // lat_count)
     vmem = pl.BlockSpec(memory_space=pltpu.VMEM)
     smem = pl.BlockSpec(memory_space=pltpu.SMEM)
+    dma = pltpu.SemaphoreType.DMA
     return pl.pallas_call(
-        spectrum_kernel,
-        out_shape=jax.ShapeDtypeStruct((L // 128, 4 * F, 128), F32),
-        in_specs=[smem, smem, vmem, vmem, vmem],
+        exchange_kernel,
+        out_shape=jax.ShapeDtypeStruct((2, 2 * time_count, F, L // time_count), F32),
+        in_specs=[smem, vmem, vmem, vmem],
         out_specs=vmem,
         scratch_shapes=[
             pltpu.VMEM((L, 128), F32),
             pltpu.VMEM((L, 128), F32),
-            pltpu.VMEM((groups * 16, 128), F32),
-            pltpu.VMEM((L, groups * 128), BF16),
-            pltpu.VMEM((4 * F, groups * 128), BF16),
+            pltpu.VMEM((lat_count * 16, 128), F32),
+            pltpu.VMEM((L, lat_count * 128), BF16),
+            pltpu.VMEM((4 * F, lat_count * 128), BF16),
+            pltpu.VMEM((time_count, lat_count, width), BF16),
+            pltpu.VMEM((lat_count * 2 * F, 128), F32),
+            pltpu.VMEM((lat_count, 2 * F, 128), BF16),
+            pltpu.VMEM((lat_count, 2 * F, 128), BF16),
+            pltpu.VMEM((time_count, 4 * F, 128), F32),
+            pltpu.VMEM((time_count, 4 * F, 128), F32),
+            dma((time_count,)), dma((time_count,)),
+            dma((lat_count,)), dma((lat_count,)),
+            dma((time_count,)), dma((time_count,)),
         ],
-        compiler_params=pltpu.CompilerParams(vmem_limit_bytes=48 << 20),
-        name="spectrum",
-    )(first_slot.reshape(1), owner_map, band, jnp.asarray(grids), jnp.asarray(steps))
+        compiler_params=pltpu.CompilerParams(
+            vmem_limit_bytes=40 << 20, collective_id=0, has_side_effects=True
+        ),
+        name="exchange",
+    )(owner_map, sent, jnp.asarray(grids), jnp.asarray(steps))
 
 
 def shards(frames, owner_map):
     lat_count = lax.axis_size("lat")
     time_count = lax.axis_size("tm")
-    orders = owner_map.shape[0]
     sent = partial_band(frames, owner_map, time_count)
     sent = sent.reshape(time_count, lat_count, 2 * F * 128)
-    parts = lax.all_to_all(sent, "tm", split_axis=0, concat_axis=0, tiled=True)
-    total = jnp.sum(parts.astype(F32), axis=0).astype(BF16).reshape(lat_count, 2 * F, 128)
-    band = lax.all_to_all(total, "lat", split_axis=0, concat_axis=0, tiled=True)
-    first_slot = lax.axis_index("lat") * (orders // lat_count) + lax.axis_index("tm") * 2
-    pieces = spectrum(band, owner_map, first_slot.astype(jnp.int32), lat_count * frames.shape[1])
-    pieces = lax.all_to_all(pieces, "tm", split_axis=0, concat_axis=0, tiled=True)
-    pieces = pieces.reshape(time_count, 2, 2, F, 128).transpose(2, 0, 1, 3, 4)
-    return pieces.reshape(2, 2 * time_count, F, 128)
+    return exchange(sent, owner_map, lat_count * frames.shape[1])
 
 
 def solution(mesh):

time: 79.5 us -> 55.8 us (0.70); the launches traced: 78.3 us -> 55.4 us
  blocking collectives: 33.5 us -> 0 us
  Pallas kernels: 21.4 us -> 51.2 us
  starting transfers between devices: 10.6 us -> 0 us
  waiting for transfers between devices: 9.06 us -> 0 us
    all_to_all x2 -> x0, blocking collectives: 33.5 us -> none  [the longest x1 23.6 us: shards(): parts = lax.all_to_all(sent, 'tm', split_axis=0, concat_axis=0, tiled=True)]
    pallas_call x1, Pallas kernels: 10.3 us -> 40.1 us  [exchange(): pl.pallas_call(exchange_kernel, out_shape=jax.ShapeDtypeStruct((2, 2 * ti...]
    all_to_all x1 -> x0, starting transfers between devices: 10.6 us -> none  [shards(): band = lax.all_to_all(total, 'lat', split_axis=0, concat_axis=0, tiled=True)]
    all_to_all x1 -> x0, waiting for transfers between devices: 9.06 us -> none  [shards(): band = lax.all_to_all(total, 'lat', split_axis=0, concat_axis=0, tiled=True)]
    unnamed x11 -> x13, local copies, waits for them, and re-layouts: 2.96 us -> 4.16 us
  transfers between devices with their start and end apart: 1 -> 0, of which waited for: 1 -> 0; matrix products, arithmetic and copies ran while one was open for 0% -> 0% of each run, Pallas kernels for 0% -> 0%
where the time goes in v1:
time: 55.8 us; the launch traced here: 55.4 us
  Pallas kernels  51.2 us (92%)
  local copies, waits for them, and re-layouts  4.16 us (7%)
    pallas_call x1, Pallas kernels, exchange(): pl.pallas_call(exchange_kernel, out_shape=jax.ShapeDtypeStruct((2, 2 * ti...  40.1 us
    pallas_call x1, Pallas kernels, partial_band(): pl.pallas_call(band_kernel, out_shape=jax.ShapeDtypeStruct((orders // 2,...  11.1 us
    unnamed x13, local copies, waits for them, and re-layouts  4.16 us

profile of v1, /device:TPU:1, one launch (start us, length us, event | category | flops | bytes accessed | tf_op | source)
XLA Modules:
  0.0 55.4 jit_solution(4612780622881915846)
XLA Ops:
  0.0 0.0 copy-start.5
  0.0 0.0 copy-start
  0.0 1.0 %copy-done = f32[8,2,16,256]{3,2,1,0:T(8,128)S(1)} copy-done((f32[8,2,16,256]{3,2,1,0:T(8,128)S(1)}, f32[8,2,16,256]{3,2,1,0:T(8,128)}, u32[]{:S(2)}) %copy-start) | copy-done | bytes 262168
  1.0 0.0 copy-start.1
  1.0 0.9 %copy-done.1 = f32[2,2,64,256]{3,2,1,0:T(8,128)S(1)} copy-done((f32[2,2,64,256]{3,2,1,0:T(8,128)S(1)}, f32[2,2,64,256]{3,2,1,0:T(8,128)}, u32[]{:S(2)}) %copy-start.1) | copy-done | bytes 262168
  1.9 0.0 copy-start.2
  1.9 0.9 %copy-done.2 = f32[2,2,32,256]{3,2,1,0:T(8,128)S(1)} copy-done((f32[2,2,32,256]{3,2,1,0:T(8,128)S(1)}, f32[2,2,32,256]{3,2,1,0:T(8,128)}, u32[]{:S(2)}) %copy-start.2) | copy-done | bytes 131096
  2.8 0.0 copy-start.4
  2.8 0.7 %copy-done.4 = s32[512]{0:T(512)S(1)} copy-done((s32[512]{0:T(512)S(1)}, s32[512]{0:T(512)}, u32[]{:S(2)}) %copy-start.4) | copy-done | bytes 2072
  3.5 0.0 copy-start.3
  3.5 11.1 %partial_band.1 = bf16[256,2048]{1,0:T(8,128)(2,1)S(1)} custom-call(s32[1]{0:T(128)} %bitcast.part_ref, bf16[16,64,4096]{2,1,0:T(8,128)(2,1)} %frames_ref.1, f32[2,2,32,256]{3,2,1,0:T(8,128)S(1)} %copy-done.2, f32[2,2,64,256]{3,2,1,0:T(8,128)S(1)} %copy-done.1, f32[8,2,16,256]{3,2,1,0:T(8,128)S(1)} %copy-done, s32[1,512]{1,0:T(1,128)S(1)} %bitcast.4), custom_call_target="tpu_custom_call" | custom-call | tf_op jit(solution)/shard_map/partial_band/pallas_call | solution.py:132
  14.6 0.0 copy-done.5
  14.6 0.0 copy-done.3
  14.6 40.1 %exchange.1 = f32[2,16,8,128]{3,2,1,0:T(8,128)S(1)} custom-call(s32[512]{0:T(512)S(1)} %copy-done.4, bf16[8,32,2048]{2,1,0:T(8,128)(2,1)S(1)} %bitcast.3, f32[3,32,128]{2,1,0:T(8,128)S(1)} %copy-done.3, f32[8,128]{1,0:T(8,128)S(1)} %copy-done.5), custom_call_target="tpu_custom_call" | custom-call | tf_op jit(solution)/shard_map/exchange/pallas_call | solution.py:386
  54.8 0.7 %copy.9 = f32[2,16,8,128]{3,2,1,0:T(8,128)} copy(f32[2,16,8,128]{3,2,1,0:T(8,128)S(1)} %exchange.1) | data formatting | bytes 262144
Async XLA Ops:
  0.0 14.6 %copy-start.5 = (f32[8,128]{1,0:T(8,128)S(1)}, f32[8,128]{1,0:T(8,128)}, u32[]{:S(2)}) copy-start(f32[8,128]{1,0:T(8,128)} %constant.20.clone.steps_ref) | copy-start | bytes 12292
  0.0 1.0 %copy-start = (f32[8,2,16,256]{3,2,1,0:T(8,128)S(1)}, f32[8,2,16,256]{3,2,1,0:T(8,128)}, u32[]{:S(2)}) copy-start(f32[8,2,16,256]{3,2,1,0:T(8,128)} %constant.18.clone.time_ref) | copy-start | bytes 786436
  1.0 0.9 %copy-start.1 = (f32[2,2,64,256]{3,2,1,0:T(8,128)S(1)}, f32[2,2,64,256]{3,2,1,0:T(8,128)}, u32[]{:S(2)}) copy-start(f32[2,2,64,256]{3,2,1,0:T(8,128)} %constant.17.clone.near_ref) | copy-start | bytes 786436
  1.9 0.9 %copy-start.2 = (f32[2,2,32,256]{3,2,1,0:T(8,128)S(1)}, f32[2,2,32,256]{3,2,1,0:T(8,128)}, u32[]{:S(2)}) copy-start(f32[2,2,32,256]{3,2,1,0:T(8,128)} %constant.16.clone.coarse_ref) | copy-start | bytes 393220
  2.8 0.7 %copy-start.4 = (s32[512]{0:T(512)S(1)}, s32[512]{0:T(512)}, u32[]{:S(2)}) copy-start(s32[512]{0:T(512)} %own_ref.1) | copy-start | bytes 6148
  3.5 11.1 %copy-start.3 = (f32[3,32,128]{2,1,0:T(8,128)S(1)}, f32[3,32,128]{2,1,0:T(8,128)}, u32[]{:S(2)}) copy-start(f32[3,32,128]{2,1,0:T(8,128)} %constant.19.clone.grids_ref) | copy-start | bytes 147460

commit v2 on v1

v2 whole, which is shorter than its diff:
```python
from functools import partial
import math

import jax
import jax.numpy as jnp
from jax import lax
from jax.experimental import pallas as pl
from jax.experimental.pallas import tpu as pltpu
from jax.sharding import PartitionSpec as P
import numpy as np

L = 1024
F = 8
BF16 = jnp.bfloat16
MESH = pl.DeviceIdType.MESH
F32 = jnp.float32


ROWS = 16
FINE = 64


def longitude_seeds(nlon, orders):
    count = nlon // 2 // FINE
    seeds = []
    for parity in range(2):
        order = np.arange(parity, orders, 2, dtype=np.int64)[None, :]
        points = np.concatenate([np.arange(count) * FINE, np.arange(FINE)])[:, None]
        angles = (points * order % nlon) * (2.0 * math.pi / nlon)
        scale = np.where(np.arange(count + FINE)[:, None] < count, math.sqrt(2.0 / nlon), 1.0)
        seeds.append(np.stack([np.cos(angles) * scale, np.sin(angles) * scale]))
    return np.stack(seeds).astype(np.float32)


def time_tables(parts, frames):
    total = parts * frames
    times = np.arange(total, dtype=np.int64)[None, :]
    frequency = (total // 8 + np.arange(F, dtype=np.int64))[:, None]
    angles = (frequency * times % total) * (2.0 * math.pi / total)
    cos_part = np.cos(angles) / math.sqrt(total)
    sin_part = np.sin(angles) / math.sqrt(total)
    real = np.concatenate([cos_part, -sin_part], axis=0)
    imag = np.concatenate([sin_part, cos_part], axis=0)
    table = np.stack([real, imag]).reshape(2, 2 * F, parts, frames).transpose(2, 0, 1, 3)
    return np.repeat(table, ROWS, axis=3).astype(np.float32)


def latitude_constants(nlat, lat_rows):
    colatitude = (np.arange(nlat // 2) + 0.5) * (math.pi / nlat)
    sine = np.sin(colatitude)
    weight = sine * (math.pi / nlat) * math.sqrt(nlat)

    def lay(values):
        values = values.reshape(-1, lat_rows // ROWS, 1, ROWS)
        return np.repeat(values, 2, axis=2).reshape(-1, 2 * lat_rows)

    steps = np.log1p(0.5 / np.arange(1, 1025)).reshape(8, 128)
    parts = [lay(np.cos(colatitude)), lay(np.log(sine)), lay(weight), steps]
    return np.concatenate(parts).astype(np.float32)


def longitude_table(seed_ref, tab_ref):
    pairs = seed_ref.shape[3]
    count = seed_ref.shape[2] - FINE
    for parity in range(2):

        def body(i, carry):
            cos_row = seed_ref[parity, 0, pl.ds(i, 1), :]
            sin_row = seed_ref[parity, 1, pl.ds(i, 1), :]
            near_cos, near_sin = seed_ref[parity, 0, count:], seed_ref[parity, 1, count:]
            at = pl.ds(pl.multiple_of(i * FINE, FINE), FINE)
            tab_ref[parity, at, :pairs] = (cos_row * near_cos - sin_row * near_sin).astype(BF16)
            tab_ref[parity, at, pairs:] = (-sin_row * near_cos - cos_row * near_sin).astype(BF16)
            return carry

        lax.fori_loop(0, count, body, 0)


def time_product_table(time_ref, wk_ref, flip):
    size = wk_ref.shape[1]
    row = lax.broadcasted_iota(jnp.int32, (ROWS, size), 0)
    lane = lax.rem(lax.broadcasted_iota(jnp.int32, (ROWS, size), 1), ROWS)
    same = row == jnp.where(flip, ROWS - 1 - lane, lane)
    for c in range(2):
        for ef in range(2 * F):
            line = jnp.broadcast_to(time_ref[c, ef : ef + 1, :], (ROWS, size))
            wk_ref[c, ef * ROWS : (ef + 1) * ROWS, :] = jnp.where(same, line, 0.0).astype(BF16)


def slot_table(own_ref, ot_ref, oh_ref, time_count, lat_count):
    orders = own_ref.shape[1]
    pairs = orders // 2
    wide = jnp.broadcast_to(own_ref[...].astype(F32), (128, orders))
    for block in range(orders // 128):
        ot_ref[block * 128 : (block + 1) * 128, :] = wide[:, block * 128 : (block + 1) * 128].T
    lane = lax.broadcasted_iota(jnp.int32, (lat_count, orders), 1)
    order = jnp.where(lane < pairs, 2 * lane, 2 * (lane - pairs) + 1).astype(F32)
    for slot in range(2):
        for peer in range(time_count):
            held = ot_ref[pl.ds(2 * peer + slot, lat_count, stride=2 * time_count), :]
            held = jnp.concatenate([held] * (orders // 128), axis=1)
            at = (slot * time_count + peer) * lat_count
            oh_ref[at : at + lat_count, :] = jnp.where(held == order, 1.0, 0.0).astype(BF16)


def degree_factors(order, rise_ref, fall_ref):
    block = 64

    def body(i, carry):
        at = pl.multiple_of(i * block, block)
        level = (at + lax.broadcasted_iota(jnp.int32, (block, 128), 0)).astype(F32)
        level_sq = level * level
        order_sq = order * order
        lower = level - 1.0
        rising = jnp.sqrt(
            jnp.maximum(4.0 * level_sq - 1.0, 0.0) / jnp.maximum(level_sq - order_sq, 1.0)
        )
        falling = jnp.sqrt(
            jnp.maximum(lower * lower - order_sq, 0.0)
            / jnp.maximum(4.0 * lower * lower - 1.0, 1.0)
        )
        rise_ref[pl.ds(at, block), :] = rising
        fall_ref[pl.ds(at, block), :] = rising * falling
        return carry

    lax.fori_loop(0, L // block, body, 0)


def diagonal(order, held, first, log_sine, weight, steps):
    step = (
        128 * lax.broadcasted_iota(jnp.int32, (8, 128), 0)
        + lax.broadcasted_iota(jnp.int32, (8, 128), 1)
        + 1
    ).astype(F32)
    sums = [jnp.sum(jnp.where(step <= m, steps, 0.0), axis=(0, 1), keepdims=True) for m in held]
    growth = jnp.where(first, sums[0], sums[1])
    lognorm = 0.5 * math.log(0.5) + 0.5 * growth + order * log_sine
    start = jnp.where(lognorm >= -60.0, jnp.exp(jnp.maximum(lognorm, -60.0)), 0.0)
    return start * weight


def fill_table(order, start, cosine, rise_ref, fall_ref, stage_ref, table_ref):
    groups = start.shape[0] // 8
    span = 16
    wide_order = jnp.broadcast_to(order, (8, 128))

    def body(i, carry):
        base = pl.multiple_of(i * span, span)
        newer, older = list(carry[0]), list(carry[1])
        for k in range(span):
            rise = jnp.broadcast_to(rise_ref[pl.ds(base + k, 1), :], (8, 128))
            fall = jnp.broadcast_to(fall_ref[pl.ds(base + k, 1), :], (8, 128))
            first = wide_order == (base + k).astype(F32)
            for g in range(groups):
                at = slice(8 * g, 8 * g + 8)
                now = (rise * cosine[at]) * newer[g] - fall * older[g]
                now = jnp.where(first, start[at], now)
                newer[g], older[g] = now, newer[g]
                stage_ref[(g * span + k) * 8 : (g * span + k) * 8 + 8, :] = now
        for g in range(groups):
            for j in range(8):
                rows = stage_ref[pl.ds(g * span * 8 + j, span, stride=8), :]
                table_ref[pl.ds(base, span), (8 * g + j) * 128 : (8 * g + j + 1) * 128] = (
                    rows.astype(BF16)
                )
        return tuple(newer), tuple(older)

    zeros = tuple(jnp.zeros((8, 128), F32) for _ in range(groups))
    lax.fori_loop(0, L // span, body, (zeros, zeros))


def run(first, last, action):
    def body(d, carry):
        action(d)
        return carry

    lax.fori_loop(first, last, body, 0)


def kernel(
    frames_ref, own_hbm, seed_hbm, time_hbm, grid_hbm, out_ref,
    image_ref, own_ref, seed_ref, time_ref, grid_ref,
    tab_ref, wk_ref, ot_ref, oh_ref, sent_ref,
    rise_ref, fall_ref, stage_ref, table_ref, both_ref,
    parts_ref, total_ref, sum_ref, away_ref, band_ref, gone_ref, degrees_ref,
    image_sem, load_sem, part_send, part_recv, lat_send, lat_recv, deg_send, deg_recv,
):
    tm, lat = lax.axis_index("tm"), lax.axis_index("lat")
    blocks, time_count, lat_count, width = parts_ref.shape
    frame_count, _, nlon = image_ref.shape[1:]
    half = nlon // 2
    pairs = seed_ref.shape[3]
    south = lat >= lat_count // 2
    north_count = lat_count // 2

    def time_peer(d):
        return lax.rem(tm + d, time_count)

    def lat_peer(d):
        return lax.rem(lat + d, lat_count)

    loads = [
        pltpu.make_async_copy(own_hbm, own_ref, load_sem.at[0]),
        pltpu.make_async_copy(seed_hbm, seed_ref, load_sem.at[1]),
        pltpu.make_async_copy(time_hbm.at[tm], time_ref, load_sem.at[2]),
        pltpu.make_async_copy(grid_hbm, grid_ref, load_sem.at[3]),
    ]
    for load in loads:
        load.start()

    def image_copy(g):
        at = pl.multiple_of(jnp.where(south, blocks - 1 - g, g) * ROWS, ROWS)
        return pltpu.make_async_copy(
            frames_ref.at[:, pl.ds(at, ROWS), :], image_ref.at[g], image_sem.at[g]
        )

    for g in range(blocks):
        image_copy(g).start()

    barrier = pltpu.get_barrier_semaphore()

    def greet_time(d):
        pl.semaphore_signal(barrier, inc=1, device_id={"tm": time_peer(d)}, device_id_type=MESH)

    def greet_lat(d):
        pl.semaphore_signal(barrier, inc=1, device_id={"lat": lat_peer(d)}, device_id_type=MESH)

    run(1, time_count, greet_time)
    run(1, lat_count, greet_lat)

    def part_copy(g, d):
        peer = time_peer(d)
        return pltpu.make_async_remote_copy(
            src_ref=sent_ref.at[g, peer], dst_ref=parts_ref.at[g, tm],
            send_sem=part_send.at[g, d], recv_sem=part_recv.at[g, tm],
            device_id={"tm": peer}, device_id_type=MESH,
        )

    def part_arrival(g, d):
        peer = time_peer(d)
        return pltpu.make_async_remote_copy(
            src_ref=sent_ref.at[g, peer], dst_ref=parts_ref.at[g, peer],
            send_sem=part_send.at[g, d], recv_sem=part_recv.at[g, peer],
            device_id={"tm": peer}, device_id_type=MESH,
        )

    def band_copy(d):
        return pltpu.make_async_remote_copy(
            src_ref=away_ref.at[lat_peer(d)], dst_ref=band_ref.at[lat],
            send_sem=lat_send.at[d], recv_sem=lat_recv.at[lat],
            device_id={"lat": lat_peer(d)}, device_id_type=MESH,
        )

    def band_arrival(d):
        peer = lat_peer(d)
        return pltpu.make_async_remote_copy(
            src_ref=away_ref.at[peer], dst_ref=band_ref.at[peer],
            send_sem=lat_send.at[d], recv_sem=lat_recv.at[peer],
            device_id={"lat": peer}, device_id_type=MESH,
        )

    def degree_copy(peer):
        return pltpu.make_async_remote_copy(
            src_ref=gone_ref.at[peer], dst_ref=degrees_ref.at[tm],
            send_sem=deg_send.at[peer], recv_sem=deg_recv.at[tm],
            device_id={"tm": peer}, device_id_type=MESH,
        )

    def degree_arrival(d):
        peer = time_peer(d)
        return pltpu.make_async_remote_copy(
            src_ref=gone_ref.at[peer], dst_ref=degrees_ref.at[peer],
            send_sem=deg_send.at[peer], recv_sem=deg_recv.at[peer],
            device_id={"tm": peer}, device_id_type=MESH,
        )

    for load in loads:
        load.wait()
    longitude_table(seed_ref, tab_ref)
    time_product_table(time_ref, wk_ref, south)
    slot_table(own_ref, ot_ref, oh_ref, time_count, lat_count)
    pl.semaphore_wait(barrier, time_count + lat_count - 2)

    def block(g):
        image_copy(g).wait()
        image = image_ref[g].reshape(frame_count * ROWS, nlon)
        first, second = image[:, :half], image[:, half:]
        bands = []
        for parity in range(2):
            folded = first + second if parity == 0 else first - second
            coef = jnp.dot(folded, tab_ref[parity], preferred_element_type=F32).astype(BF16)
            part = jnp.dot(wk_ref[0], coef[:, :pairs], preferred_element_type=F32)
            part = part + jnp.dot(wk_ref[1], coef[:, pairs:], preferred_element_type=F32)
            bands.append(part.astype(BF16))
        both = jnp.concatenate(bands, axis=1)
        moved = lax.dot_general(
            oh_ref[...], both, (((1,), (1,)), ((), ())), preferred_element_type=F32
        ).astype(BF16)
        for slot in range(2):
            sent_ref[g, :, :, slot * width // 2 : (slot + 1) * width // 2] = moved[
                slot * pairs : (slot + 1) * pairs
            ].reshape(time_count, lat_count, width // 2)
        run(1, time_count, lambda d: part_copy(g, d).start())

    run(0, blocks, block)

    slot = lat * (2 * time_count) + tm * 2
    held = [ot_ref[pl.ds(slot + s, 1), :] for s in range(2)]
    lane = lax.broadcasted_iota(jnp.int32, (1, 128), 1)
    first_slot = lax.rem(lane // ROWS, 2) == 0
    order = jnp.where(first_slot, held[0], held[1])
    degree_factors(order, rise_ref, fall_ref)
    cosine, log_sine, weight = (
        grid_ref[i * north_count : (i + 1) * north_count] for i in range(3)
    )
    steps = grid_ref[3 * north_count : 3 * north_count + 8]
    start = diagonal(order, held, first_slot, log_sine, weight, steps)
    fill_table(order, start, cosine, rise_ref, fall_ref, stage_ref, table_ref)

    def collect(g):
        run(1, time_count, lambda d: part_arrival(g, d).wait_recv())
        total = sent_ref[g, tm].astype(F32)
        for d in range(1, time_count):
            total = total + parts_ref[g, time_peer(d)].astype(F32)
        total_ref[g] = total

    run(0, blocks, collect)
    for ef in range(2 * F):
        pieces = [
            total_ref[g, :, s * width // 2 + ef * ROWS : s * width // 2 + (ef + 1) * ROWS]
            for g in range(blocks)
            for s in range(2)
        ]
        sum_ref[pl.ds(ef, lat_count, stride=2 * F), :] = jnp.concatenate(pieces, axis=1)
    away_ref[...] = sum_ref[...].astype(BF16).reshape(away_ref.shape)
    run(1, lat_count, lambda d: band_copy(d).start())
    band_ref[lat] = away_ref[lat]
    run(1, lat_count, lambda d: band_arrival(d).wait_recv())

    lanes = lax.broadcasted_iota(jnp.int32, (2 * F, 128), 1)
    mine = lax.rem(lanes // ROWS, 2) == 0
    for j in range(north_count):
        north = band_ref[j].astype(F32)
        mirror = band_ref[lat_count - 1 - j].astype(F32)
        at = slice(j * 128, (j + 1) * 128)
        for sign, tile in enumerate((north + mirror, north - mirror)):
            base = sign * 4 * F
            both_ref[base : base + 2 * F, at] = jnp.where(mine, tile, 0.0).astype(BF16)
            both_ref[base + 2 * F : base + 4 * F, at] = jnp.where(mine, 0.0, tile).astype(BF16)

    def product(d):
        pair = lax.rem(tm // 2 + d, time_count // 2)
        base = pl.multiple_of(pair * 256, 256)
        piece = lax.dot_general(
            both_ref[...],
            table_ref[pl.ds(base, 256), :],
            (((1,), (1,)), ((), ())),
            preferred_element_type=F32,
        )
        level = (base + lax.broadcasted_iota(jnp.int32, (2 * F, 256), 1)).astype(F32)
        for s in range(2):
            offset = level + held[s][:, :1]
            odd = offset - 2.0 * jnp.floor(offset * 0.5)
            at = slice(2 * F * s, 2 * F * (s + 1))
            even_part, odd_part = piece[at], piece[4 * F + 2 * F * s : 4 * F + 2 * F * (s + 1)]
            chosen = jnp.where(odd == 0.0, even_part, odd_part)
            for k in range(2):
                gone_ref[2 * pair + k, at] = chosen[:, k * 128 : (k + 1) * 128]
        for k in range(2):
            peer = 2 * pair + k

            @pl.when(peer != tm)
            def _():
                degree_copy(peer).start()

    run(1, time_count // 2 + 1, product)
    degrees_ref[tm] = gone_ref[tm]
    run(1, time_count, lambda d: degree_arrival(d).wait_recv())
    for peer in range(time_count):
        for s in range(2):
            for e in range(2):
                at = (2 * s + e) * F
                out_ref[e, 2 * peer + s] = degrees_ref[peer, at : at + F, :]
    run(0, blocks, lambda g: run(1, time_count, lambda d: part_copy(g, d).wait_send()))
    run(1, lat_count, lambda d: band_copy(d).wait_send())
    run(1, time_count, lambda d: degree_copy(time_peer(d)).wait_send())


def shards(frames, owner_map):
    lat_count = lax.axis_size("lat")
    time_count = lax.axis_size("tm")
    frame_count, lat_rows, nlon = frames.shape
    orders = owner_map.shape[0]
    blocks = lat_rows // ROWS
    size = frame_count * ROWS
    width = 2 * 2 * F * ROWS
    seeds = longitude_seeds(nlon, orders)
    times = time_tables(time_count, frame_count)
    grids = latitude_constants(lat_count * lat_rows, lat_rows)
    hbm = pl.BlockSpec(memory_space=pltpu.HBM)
    dma = pltpu.SemaphoreType.DMA
    return pl.pallas_call(
        kernel,
        out_shape=jax.ShapeDtypeStruct((2, 2 * time_count, F, L // time_count), F32),
        in_specs=[hbm] * 5,
        out_specs=pl.BlockSpec(memory_space=pltpu.VMEM),
        scratch_shapes=[
            pltpu.VMEM((blocks, frame_count, ROWS, nlon), BF16),
            pltpu.VMEM((1, orders), jnp.int32),
            pltpu.VMEM(seeds.shape, F32),
            pltpu.VMEM(times.shape[1:], F32),
            pltpu.VMEM(grids.shape, F32),
            pltpu.VMEM((2, nlon // 2, orders), BF16),
            pltpu.VMEM((2, size, size), BF16),
            pltpu.VMEM((orders, 128), F32),
            pltpu.VMEM((orders, orders), BF16),
            pltpu.VMEM((blocks, time_count, lat_count, width), BF16),
            pltpu.VMEM((L, 128), F32),
            pltpu.VMEM((L, 128), F32),
            pltpu.VMEM((lat_count * 8, 128), F32),
            pltpu.VMEM((L, lat_count * 64), BF16),
            pltpu.VMEM((8 * F, lat_count * 64), BF16),
            pltpu.VMEM((blocks, time_count, lat_count, width), BF16),
            pltpu.VMEM((blocks, lat_count, width), F32),
            pltpu.VMEM((lat_count * 2 * F, 128), F32),
            pltpu.VMEM((lat_count, 2 * F, 128), BF16),
            pltpu.VMEM((lat_count, 2 * F, 128), BF16),
            pltpu.VMEM((time_count, 4 * F, 128), F32),
            pltpu.VMEM((time_count, 4 * F, 128), F32),
            dma((blocks,)), dma((4,)),
            dma((blocks, time_count)), dma((blocks, time_count)),
            dma((lat_count,)), dma((lat_count,)),
            dma((time_count,)), dma((time_count,)),
        ],
        compiler_params=pltpu.CompilerParams(
            vmem_limit_bytes=56 << 20, collective_id=0, has_side_effects=True
        ),
        name="spectrum",
    )(
        frames, owner_map.reshape(1, orders),
        jnp.asarray(seeds), jnp.asarray(times), jnp.asarray(grids),
    )


def solution(mesh):
    return jax.shard_map(
        shards,
        mesh=mesh,
        in_specs=(P("tm", "lat", None), P()),
        out_specs=P(None, "lat", None, "tm"),
        check_vma=False,
    )
```

time: 55.8 us -> 44.1 us (0.79)
  Pallas kernels: 51.2 us -> 42.5 us
  local copies, waits for them, and re-layouts: 4.16 us -> 1.57 us
    pallas_call x2 -> x1, Pallas kernels: 51.2 us -> 42.5 us  [shards(): pl.pallas_call(kernel, out_shape=jax.ShapeDtypeStruct((2, 2 * time_count,...]
    unnamed x13 -> x1, local copies, waits for them, and re-layouts: 4.16 us -> 1.57 us
where the time goes in v2:
time: 44.1 us; the launch traced here: 44 us
  Pallas kernels  42.5 us (96%)
  local copies, waits for them, and re-layouts  1.57 us (4%)
    pallas_call x1, Pallas kernels, shards(): pl.pallas_call(kernel, out_shape=jax.ShapeDtypeStruct((2, 2 * time_count,...  42.5 us
    unnamed x1, local copies, waits for them, and re-layouts  1.57 us

profile of v2, /device:TPU:1, one launch (start us, length us, event | category | flops | bytes accessed | tf_op | source)
XLA Modules:
  0.0 44.0 jit_solution(5279560888407196556)
XLA Ops:
  0.0 42.5 %spectrum.1 = f32[2,16,8,128]{3,2,1,0:T(8,128)} custom-call(bf16[16,64,4096]{2,1,0:T(8,128)(2,1)} %frames_ref.1, s32[1,512]{1,0:T(1,128)} %bitcast.1, f32[2,2,96,256]{3,2,1,0:T(8,128)} %constant.6.clone.seed_hbm, f32[8,2,16,256]{3,2,1,0:T(8,128)} %constant.7.clone.time_hbm, f32[56,128]{1,0:T(8,128)} %constant.8.clone.grid_hbm), custom_call_target="tpu_custom_call" | custom-call | tf_op jit(solution)/shard_map/spectrum/pallas_call | solution.py:402
  42.5 1.6 %copy.7 = f32[2,16,8,128]{3,2,1,0:T(8,128)} copy(f32[2,16,8,128]{3,2,1,0:T(8,128)} %spectrum.1) | data formatting | bytes 262144

commit v3 on v2

--- a/solution.py
+++ b/solution.py
@@ -51,8 +51,9 @@
     weight = sine * (math.pi / nlat) * math.sqrt(nlat)
 
     def lay(values):
-        values = values.reshape(-1, lat_rows // ROWS, 1, ROWS)
-        return np.repeat(values, 2, axis=2).reshape(-1, 2 * lat_rows)
+        values = values.reshape(-1, 2, 2, lat_rows // ROWS // 2, 1, ROWS)
+        values = np.repeat(values.transpose(2, 0, 1, 3, 4, 5), 2, axis=4)
+        return values.reshape(-1, 2 * lat_rows)
 
     steps = np.log1p(0.5 / np.arange(1, 1025)).reshape(8, 128)
     parts = [lay(np.cos(colatitude)), lay(np.log(sine)), lay(weight), steps]
@@ -174,14 +175,18 @@
         action(d)
         return carry
 
-    lax.fori_loop(first, last, body, 0)
+    if last - first < 8:
+        for d in range(first, last):
+            action(d)
+    else:
+        lax.fori_loop(first, last, body, 0)
 
 
 def kernel(
     frames_ref, own_hbm, seed_hbm, time_hbm, grid_hbm, out_ref,
     image_ref, own_ref, seed_ref, time_ref, grid_ref,
     tab_ref, wk_ref, ot_ref, oh_ref, sent_ref,
-    rise_ref, fall_ref, stage_ref, table_ref, both_ref,
+    rise_ref, fall_ref, stage_ref, table_ref, both_ref, acc_ref,
     parts_ref, total_ref, sum_ref, away_ref, band_ref, gone_ref, degrees_ref,
     image_sem, load_sem, part_send, part_recv, lat_send, lat_recv, deg_send, deg_recv,
 ):
@@ -193,11 +198,14 @@
     south = lat >= lat_count // 2
     north_count = lat_count // 2
 
+    def wrap(value, count):
+        return jnp.where(value >= count, value - count, value)
+
     def time_peer(d):
-        return lax.rem(tm + d, time_count)
+        return wrap(tm + d, time_count)
 
     def lat_peer(d):
-        return lax.rem(lat + d, lat_count)
+        return wrap(lat + d, lat_count)
 
     loads = [
         pltpu.make_async_copy(own_hbm, own_ref, load_sem.at[0]),
@@ -244,18 +252,19 @@
             device_id={"tm": peer}, device_id_type=MESH,
         )
 
-    def band_copy(d):
-        return pltpu.make_async_remote_copy(
-            src_ref=away_ref.at[lat_peer(d)], dst_ref=band_ref.at[lat],
-            send_sem=lat_send.at[d], recv_sem=lat_recv.at[lat],
-            device_id={"lat": lat_peer(d)}, device_id_type=MESH,
-        )
-
-    def band_arrival(d):
+    def band_copy(h, d):
         peer = lat_peer(d)
         return pltpu.make_async_remote_copy(
-            src_ref=away_ref.at[peer], dst_ref=band_ref.at[peer],
-            send_sem=lat_send.at[d], recv_sem=lat_recv.at[peer],
+            src_ref=away_ref.at[h, peer], dst_ref=band_ref.at[h, lat],
+            send_sem=lat_send.at[h, d], recv_sem=lat_recv.at[h, lat],
+            device_id={"lat": peer}, device_id_type=MESH,
+        )
+
+    def band_arrival(h, d):
+        peer = lat_peer(d)
+        return pltpu.make_async_remote_copy(
+            src_ref=away_ref.at[h, peer], dst_ref=band_ref.at[h, peer],
+            send_sem=lat_send.at[h, d], recv_sem=lat_recv.at[h, peer],
             device_id={"lat": peer}, device_id_type=MESH,
         )
 
@@ -302,7 +311,7 @@
             ].reshape(time_count, lat_count, width // 2)
         run(1, time_count, lambda d: part_copy(g, d).start())
 
-    run(0, blocks, block)
+    lax.fori_loop(0, blocks, lambda g, carry: (block(g), carry)[1], 0)
 
     slot = lat * (2 * time_count) + tm * 2
     held = [ot_ref[pl.ds(slot + s, 1), :] for s in range(2)]
@@ -324,39 +333,67 @@
             total = total + parts_ref[g, time_peer(d)].astype(F32)
         total_ref[g] = total
 
-    run(0, blocks, collect)
-    for ef in range(2 * F):
-        pieces = [
-            total_ref[g, :, s * width // 2 + ef * ROWS : s * width // 2 + (ef + 1) * ROWS]
-            for g in range(blocks)
-            for s in range(2)
-        ]
-        sum_ref[pl.ds(ef, lat_count, stride=2 * F), :] = jnp.concatenate(pieces, axis=1)
-    away_ref[...] = sum_ref[...].astype(BF16).reshape(away_ref.shape)
-    run(1, lat_count, lambda d: band_copy(d).start())
-    band_ref[lat] = away_ref[lat]
-    run(1, lat_count, lambda d: band_arrival(d).wait_recv())
-
-    lanes = lax.broadcasted_iota(jnp.int32, (2 * F, 128), 1)
+    def send_half(h):
+        held_blocks = range(h * blocks // 2, (h + 1) * blocks // 2)
+        for g in held_blocks:
+            collect(g)
+        for low in range(F):
+            pieces = [
+                total_ref[g, :, base + ef * ROWS : base + (ef + 1) * ROWS]
+                for ef in (low, low + F)
+                for g in held_blocks
+                for base in (0, width // 2)
+            ]
+            sum_ref[pl.ds(low, lat_count, stride=F), :] = jnp.concatenate(pieces, axis=1)
+        away_ref[h] = sum_ref[...].astype(BF16).reshape(away_ref.shape[1:])
+        run(1, lat_count, lambda d: band_copy(h, d).start())
+        band_ref[h, lat] = away_ref[h, lat]
+
+    for h in range(2):
+        send_half(h)
+
+    lanes = lax.broadcasted_iota(jnp.int32, (F, 128), 1)
     mine = lax.rem(lanes // ROWS, 2) == 0
-    for j in range(north_count):
-        north = band_ref[j].astype(F32)
-        mirror = band_ref[lat_count - 1 - j].astype(F32)
-        at = slice(j * 128, (j + 1) * 128)
-        for sign, tile in enumerate((north + mirror, north - mirror)):
-            base = sign * 4 * F
-            both_ref[base : base + 2 * F, at] = jnp.where(mine, tile, 0.0).astype(BF16)
-            both_ref[base + 2 * F : base + 4 * F, at] = jnp.where(mine, 0.0, tile).astype(BF16)
-
-    def product(d):
-        pair = lax.rem(tm // 2 + d, time_count // 2)
-        base = pl.multiple_of(pair * 256, 256)
-        piece = lax.dot_general(
-            both_ref[...],
-            table_ref[pl.ds(base, 256), :],
+
+    def receive_half(h):
+        run(1, lat_count, lambda d: band_arrival(h, d).wait_recv())
+        for pair in range(north_count // 2):
+            north = [band_ref[h, 2 * pair + k].astype(F32) for k in range(2)]
+            mirror = [band_ref[h, lat_count - 1 - 2 * pair - k].astype(F32) for k in range(2)]
+            at = slice((h * north_count // 2 + pair) * 128, (h * north_count // 2 + pair + 1) * 128)
+            for sign in range(2):
+                tiles = [n - m if sign else n + m for n, m in zip(north, mirror)]
+                parts = [
+                    jnp.concatenate([tile[:, k * 64 : (k + 1) * 64] for tile in tiles], axis=1)
+                    for k in range(2)
+                ]
+                whole = jnp.concatenate(parts, axis=0)
+                both_mine = jnp.concatenate([mine, mine], axis=0)
+                base = sign * 4 * F
+                both_ref[base : base + 2 * F, at] = jnp.where(both_mine, whole, 0.0).astype(BF16)
+                both_ref[base + 2 * F : base + 4 * F, at] = jnp.where(
+                    both_mine, 0.0, whole
+                ).astype(BF16)
+
+    depth = both_ref.shape[1] // 2
+
+    def half_product(h, base):
+        return lax.dot_general(
+            both_ref[:, h * depth : (h + 1) * depth],
+            table_ref[pl.ds(base, 256), h * depth : (h + 1) * depth],
             (((1,), (1,)), ((), ())),
             preferred_element_type=F32,
         )
+
+    receive_half(0)
+    for base in range(0, L, 256):
+        acc_ref[base // 256] = half_product(0, base)
+    receive_half(1)
+
+    def product(d):
+        pair = wrap(tm // 2 + d, time_count // 2)
+        base = pl.multiple_of(pair * 256, 256)
+        piece = acc_ref[pair] + half_product(1, base)
         level = (base + lax.broadcasted_iota(jnp.int32, (2 * F, 256), 1)).astype(F32)
         for s in range(2):
             offset = level + held[s][:, :1]
@@ -373,7 +410,8 @@
             def _():
                 degree_copy(peer).start()
 
-    run(1, time_count // 2 + 1, product)
+    for d in range(1, time_count // 2 + 1):
+        product(d)
     degrees_ref[tm] = gone_ref[tm]
     run(1, time_count, lambda d: degree_arrival(d).wait_recv())
     for peer in range(time_count):
@@ -382,7 +420,8 @@
                 at = (2 * s + e) * F
                 out_ref[e, 2 * peer + s] = degrees_ref[peer, at : at + F, :]
     run(0, blocks, lambda g: run(1, time_count, lambda d: part_copy(g, d).wait_send()))
-    run(1, lat_count, lambda d: band_copy(d).wait_send())
+    for h in range(2):
+        run(1, lat_count, lambda d: band_copy(h, d).wait_send())
     run(1, time_count, lambda d: degree_copy(time_peer(d)).wait_send())
 
 
@@ -420,16 +459,17 @@
             pltpu.VMEM((lat_count * 8, 128), F32),
             pltpu.VMEM((L, lat_count * 64), BF16),
             pltpu.VMEM((8 * F, lat_count * 64), BF16),
+            pltpu.VMEM((L // 256, 8 * F, 256), F32),
             pltpu.VMEM((blocks, time_count, lat_count, width), BF16),
             pltpu.VMEM((blocks, lat_count, width), F32),
-            pltpu.VMEM((lat_count * 2 * F, 128), F32),
-            pltpu.VMEM((lat_count, 2 * F, 128), BF16),
-            pltpu.VMEM((lat_count, 2 * F, 128), BF16),
+            pltpu.VMEM((lat_count * F, 128), F32),
+            pltpu.VMEM((2, lat_count, F, 128), BF16),
+            pltpu.VMEM((2, lat_count, F, 128), BF16),
             pltpu.VMEM((time_count, 4 * F, 128), F32),
             pltpu.VMEM((time_count, 4 * F, 128), F32),
             dma((blocks,)), dma((4,)),
             dma((blocks, time_count)), dma((blocks, time_count)),
-            dma((lat_count,)), dma((lat_count,)),
+            dma((2, lat_count)), dma((2, lat_count)),
             dma((time_count,)), dma((time_count,)),
         ],
         compiler_params=pltpu.CompilerParams(

time: 44.1 us -> 42.9 us (0.973)
  Pallas kernels: 42.5 us -> 41.3 us
    pallas_call x1, Pallas kernels: 42.5 us -> 41.3 us  [shards(): pl.pallas_call(kernel, out_shape=jax.ShapeDtypeStruct((2, 2 * time_count,...]
where the time goes in v3:
time: 42.9 us; the launch traced here: 42.8 us
  Pallas kernels  41.3 us (96%)
  local copies, waits for them, and re-layouts  1.57 us (4%)
    pallas_call x1, Pallas kernels, shards(): pl.pallas_call(kernel, out_shape=jax.ShapeDtypeStruct((2, 2 * time_count,...  41.3 us
    unnamed x1, local copies, waits for them, and re-layouts  1.57 us

profile of v3, /device:TPU:1, one launch (start us, length us, event | category | flops | bytes accessed | tf_op | source)
XLA Modules:
  0.0 42.8 jit_solution(9855187682974482255)
XLA Ops:
  0.0 41.3 %spectrum.1 = f32[2,16,8,128]{3,2,1,0:T(8,128)} custom-call(bf16[16,64,4096]{2,1,0:T(8,128)(2,1)} %frames_ref.1, s32[1,512]{1,0:T(1,128)} %bitcast.1, f32[2,2,96,256]{3,2,1,0:T(8,128)} %constant.6.clone.seed_hbm, f32[8,2,16,256]{3,2,1,0:T(8,128)} %constant.7.clone.time_hbm, f32[56,128]{1,0:T(8,128)} %constant.8.clone.grid_hbm), custom_call_target="tpu_custom_call" | custom-call | tf_op jit(solution)/shard_map/spectrum/pallas_call | solution.py:441
  41.3 1.6 %copy.7 = f32[2,16,8,128]{3,2,1,0:T(8,128)} copy(f32[2,16,8,128]{3,2,1,0:T(8,128)} %spectrum.1) | data formatting | bytes 262144

commit v4 on v3

--- a/solution.py
+++ b/solution.py
@@ -17,6 +17,7 @@
 
 
 ROWS = 16
+ORDER = ((2, 1), (1, 1), (3, 1), (0, 1), (2, 0), (1, 0), (3, 0))
 FINE = 64
 
 
@@ -179,7 +180,7 @@
         for d in range(first, last):
             action(d)
     else:
-        lax.fori_loop(first, last, body, 0)
+        lax.fori_loop(first, last, body, 0, unroll=True)
 
 
 def kernel(
@@ -222,8 +223,7 @@
             frames_ref.at[:, pl.ds(at, ROWS), :], image_ref.at[g], image_sem.at[g]
         )
 
-    for g in range(blocks):
-        image_copy(g).start()
+    image_copy(0).start()
 
     barrier = pltpu.get_barrier_semaphore()
 
@@ -236,8 +236,16 @@
     run(1, time_count, greet_time)
     run(1, lat_count, greet_lat)
 
+    ring = time_count // 2
+    row = jnp.where(tm >= ring, 1, 0)
+    column = tm - row * ring
+
+    def part_peer(d):
+        dx, dy = ORDER[d - 1]
+        return (1 - row if dy else row) * ring + wrap(column + dx, ring)
+
     def part_copy(g, d):
-        peer = time_peer(d)
+        peer = part_peer(d)
         return pltpu.make_async_remote_copy(
             src_ref=sent_ref.at[g, peer], dst_ref=parts_ref.at[g, tm],
             send_sem=part_send.at[g, d], recv_sem=part_recv.at[g, tm],
@@ -245,7 +253,7 @@
         )
 
     def part_arrival(g, d):
-        peer = time_peer(d)
+        peer = part_peer(d)
         return pltpu.make_async_remote_copy(
             src_ref=sent_ref.at[g, peer], dst_ref=parts_ref.at[g, peer],
             send_sem=part_send.at[g, d], recv_sem=part_recv.at[g, peer],
@@ -292,6 +300,11 @@
 
     def block(g):
         image_copy(g).wait()
+
+        @pl.when(g + 1 < blocks)
+        def _():
+            image_copy(g + 1).start()
+
         image = image_ref[g].reshape(frame_count * ROWS, nlon)
         first, second = image[:, :half], image[:, half:]
         bands = []
@@ -330,7 +343,7 @@
         run(1, time_count, lambda d: part_arrival(g, d).wait_recv())
         total = sent_ref[g, tm].astype(F32)
         for d in range(1, time_count):
-            total = total + parts_ref[g, time_peer(d)].astype(F32)
+            total = total + parts_ref[g, part_peer(d)].astype(F32)
         total_ref[g] = total
 
     def send_half(h):

time: 42.9 us -> 41.4 us (0.965)
  Pallas kernels: 41.3 us -> 39.7 us
    pallas_call x1, Pallas kernels: 41.3 us -> 39.7 us  [shards(): pl.pallas_call(kernel, out_shape=jax.ShapeDtypeStruct((2, 2 * time_count,...]
where the time goes in v4:
time: 41.4 us; the launch traced here: 41.3 us
  Pallas kernels  39.7 us (96%)
  local copies, waits for them, and re-layouts  1.57 us (4%)
    pallas_call x1, Pallas kernels, shards(): pl.pallas_call(kernel, out_shape=jax.ShapeDtypeStruct((2, 2 * time_count,...  39.7 us
    unnamed x1, local copies, waits for them, and re-layouts  1.57 us

profile of v4, /device:TPU:1, one launch (start us, length us, event | category | flops | bytes accessed | tf_op | source)
XLA Modules:
  0.0 41.3 jit_solution(3048745206114538461)
XLA Ops:
  0.0 39.7 %spectrum.1 = f32[2,16,8,128]{3,2,1,0:T(8,128)} custom-call(bf16[16,64,4096]{2,1,0:T(8,128)(2,1)} %frames_ref.1, s32[1,512]{1,0:T(1,128)} %bitcast.1, f32[2,2,96,256]{3,2,1,0:T(8,128)} %constant.6.clone.seed_hbm, f32[8,2,16,256]{3,2,1,0:T(8,128)} %constant.7.clone.time_hbm, f32[56,128]{1,0:T(8,128)} %constant.8.clone.grid_hbm), custom_call_target="tpu_custom_call" | custom-call | tf_op jit(solution)/shard_map/spectrum/pallas_call | solution.py:454
  39.7 1.6 %copy.7 = f32[2,16,8,128]{3,2,1,0:T(8,128)} copy(f32[2,16,8,128]{3,2,1,0:T(8,128)} %spectrum.1) | data formatting | bytes 262144

commit v5 on v4

--- a/solution.py
+++ b/solution.py
@@ -359,7 +359,9 @@
             ]
             sum_ref[pl.ds(low, lat_count, stride=F), :] = jnp.concatenate(pieces, axis=1)
         away_ref[h] = sum_ref[...].astype(BF16).reshape(away_ref.shape[1:])
-        run(1, lat_count, lambda d: band_copy(h, d).start())
+        span = lat_count // 4
+        for d in sorted(range(1, lat_count), key=lambda d: -min(d // 2 % span, -(d // 2) % span)):
+            band_copy(h, d).start()
         band_ref[h, lat] = away_ref[h, lat]
 
     for h in range(2):

time: 41.4 us -> 41.2 us (level)
  no operation moved by 1% of the time
where the time goes in v5:
time: 41.2 us; the launch traced here: 41 us
  Pallas kernels  39.5 us (96%)
  local copies, waits for them, and re-layouts  1.57 us (4%)
    pallas_call x1, Pallas kernels, shards(): pl.pallas_call(kernel, out_shape=jax.ShapeDtypeStruct((2, 2 * time_count,...  39.5 us
    unnamed x1, local copies, waits for them, and re-layouts  1.57 us

profile of v5, /device:TPU:1, one launch (start us, length us, event | category | flops | bytes accessed | tf_op | source)
XLA Modules:
  0.0 41.0 jit_solution(17343702044574034477)
XLA Ops:
  0.0 39.5 %spectrum.1 = f32[2,16,8,128]{3,2,1,0:T(8,128)} custom-call(bf16[16,64,4096]{2,1,0:T(8,128)(2,1)} %frames_ref.1, s32[1,512]{1,0:T(1,128)} %bitcast.1, f32[2,2,96,256]{3,2,1,0:T(8,128)} %constant.6.clone.seed_hbm, f32[8,2,16,256]{3,2,1,0:T(8,128)} %constant.7.clone.time_hbm, f32[56,128]{1,0:T(8,128)} %constant.8.clone.grid_hbm), custom_call_target="tpu_custom_call" | custom-call | tf_op jit(solution)/shard_map/spectrum/pallas_call | solution.py:456
  39.5 1.6 %copy.7 = f32[2,16,8,128]{3,2,1,0:T(8,128)} copy(f32[2,16,8,128]{3,2,1,0:T(8,128)} %spectrum.1) | data formatting | bytes 262144
